TPU v7x, 32 devices: a whole 2x2x4 slice. The times are simulated.
32 devices in a mesh: ex: 4 (over z), ft: 8 (over y, x, core).
Axes of the slice: x: 2, y: 2, z: 4, core: 2. Of those that a mesh axis runs over, the one named last changes fastest.
Arguments:
- tiles: bfloat16 [3072, 128, 128], P(('ex', 'ft')), may hold values from -0.5 to 0.5
- tile_count: int32 [32], P(('ex', 'ft')), may hold values from 16 to 96, as said below
- tile_cslot: int32 [3072], P(('ex', 'ft')), may hold values from 0 to 31
- tile_rslot: int32 [3072], P(('ex', 'ft')), may hold values from 0 to 31
- need_cols: int32 [32, 4, 8], P(('ex', 'ft')), may hold values from 0 to 127
- fold_rows: int32 [32, 8, 4], P(('ex', 'ft')), may hold values from 0 to 7
- weights: float32 [64, 4, 128], P('ft', 'ex'), may hold values from 0.01 to 0.25
- directions: float32 [512, 8, 2, 128], P('ex', 'ft'), may hold values from -6 to 6
Outputs:
- hessvec: float32 [512, 8, 2, 128], P('ex', 'ft')
Inputs may be any that keep to these rules, and one draw needn't show every extreme that they name: tile_count reaches 96 on some device in every draw; the mean is about a third of that.
All inputs are finite; a program needn't handle non-finite values.
Results may differ from a plain program's by a relative error of at most 0.0024.
Values may be sent and summed in bfloat16 or wider, within the bound.
A program may use at most 64 MiB of HBM per device.

v0:
```python
import jax
import jax.numpy as jnp
from jax import lax
from jax.sharding import PartitionSpec as P

batch_tiles = 16
scale_back = 4.0


def tile_pass(tiles, slot_in, slot_out, live_count, source, out_rows, forward):
    tile_side = tiles.shape[1]
    num_vecs = source.shape[1]
    blocks = (live_count + batch_tiles - 1) // batch_tiles
    offsets = jnp.arange(batch_tiles, dtype=jnp.int32)

    def advance(index, running):
        start = index * batch_tiles
        tile_group = lax.dynamic_slice_in_dim(tiles, start, batch_tiles, 0)
        pick_slots = lax.dynamic_slice_in_dim(slot_in, start, batch_tiles, 0)
        put_slots = lax.dynamic_slice_in_dim(slot_out, start, batch_tiles, 0)
        inputs = source[pick_slots]
        if forward:
            result = jnp.einsum(
                "tij,tkj->tki", tile_group, inputs, preferred_element_type=jnp.float32
            )
        else:
            result = jnp.einsum(
                "tij,tki->tkj", tile_group, inputs, preferred_element_type=jnp.float32
            )
        live_mask = start + offsets < live_count
        result = jnp.where(live_mask[:, None, None], result, jnp.zeros_like(result))
        return running.at[put_slots].add(result)

    return lax.fori_loop(
        0, blocks, advance, jnp.zeros((out_rows, num_vecs, tile_side), jnp.float32)
    )


def local(tiles, tile_count, tile_cslot, tile_rslot, need_cols, fold_rows, weights, directions):
    tile_side = tiles.shape[1]
    ex_size = lax.axis_size("ex")
    ft_size = lax.axis_size("ft")
    col_blocks = directions.shape[0]
    num_vecs = directions.shape[2]
    row_blocks = weights.shape[0]
    live_count = tile_count[0]
    own_vec = directions.reshape(col_blocks, num_vecs, tile_side)
    own_bf = own_vec.astype(jnp.bfloat16)
    requested = need_cols[0]
    rows_listed = fold_rows[0]
    row_map = (jnp.arange(ft_size, dtype=jnp.int32)[:, None] * row_blocks + rows_listed).reshape(-1)
    col_map = (jnp.arange(ex_size, dtype=jnp.int32)[:, None] * col_blocks + requested).reshape(-1)
    whole_group = lax.all_gather(own_bf, "ex", axis=0, tiled=True)
    column_in = whole_group[col_map]
    margin_part = tile_pass(
        tiles, tile_cslot, tile_rslot, live_count, column_in, row_map.shape[0], True
    )
    own_weight = weights.reshape(row_blocks, tile_side)
    owned_lists = lax.all_to_all(rows_listed, "ft", split_axis=0, concat_axis=0, tiled=True)
    pieces = margin_part.reshape(ft_size, -1, num_vecs, tile_side)
    arrived_rows = lax.all_to_all(pieces, "ft", split_axis=0, concat_axis=0, tiled=True)
    owned_flat = owned_lists.reshape(-1)
    margins = (
        jnp.zeros((row_blocks, num_vecs, tile_side), jnp.float32)
        .at[owned_flat]
        .add(arrived_rows.reshape(-1, num_vecs, tile_side))
    )
    own_scaled = (own_weight[:, None, :] * margins).astype(jnp.bfloat16)
    reply = own_scaled[owned_flat].reshape(ft_size, -1, num_vecs, tile_side)
    returned = lax.all_to_all(reply, "ft", split_axis=0, concat_axis=0, tiled=True)
    row_in = returned.reshape(-1, num_vecs, tile_side)
    column_part = tile_pass(
        tiles, tile_rslot, tile_cslot, live_count, row_in, col_map.shape[0], False
    )
    spread_cols = (
        jnp.zeros((col_blocks * ex_size, num_vecs, tile_side), jnp.float32)
        .at[col_map]
        .add(column_part)
    )
    curvature = lax.psum_scatter(spread_cols, "ex", scatter_dimension=0, tiled=True)
    hessian_part = own_vec + scale_back * curvature
    return hessian_part.reshape(directions.shape)


def solution(mesh):
    return jax.shard_map(
        local,
        mesh=mesh,
        in_specs=(
            P(("ex", "ft"), None, None),
            P(("ex", "ft")),
            P(("ex", "ft")),
            P(("ex", "ft")),
            P(("ex", "ft"), None, None),
            P(("ex", "ft"), None, None),
            P("ft", "ex", None),
            P("ex", "ft", None, None),
        ),
        out_specs=P("ex", "ft", None, None),
        check_vma=False,
    )
```

profile of v0, /device:TPU:0, one launch (start us, length us, event | category | flops | bytes accessed | tf_op | source)
XLA Modules:
  0.0 159.1 jit_solution(9264948433535837132)
XLA Ops:
  6.5 1.4 copy.11
  7.9 5.2 %all-to-all-start = ((s32[8,1,4]{2,1,0:T(1,128)}), s32[8,1,4]{2,1,0:T(1,128)S(1)}, u32[]{:S(2)}, u32[]{:S(2)}) async-start(s32[8,1,4]{2,1,0:T(1,128)} %copy.11), calls=%async_computation | async-start | bytes 8192 | tf_op jit(solution)/shard_map/all_to_all | solution.py:59
  13.9 0.8 squeeze.7
  14.7 1.0 bitcast_convert_fusion
  15.7 14.3 %all_gather.3 = bf16[512,2,128]{2,1,0:T(2,128)(2,1)S(1)} all-gather(bf16[128,2,128]{2,1,0:T(2,128)(2,1)S(1)} %bitcast_convert_fusion), channel_id=1, replica_groups=mesh['ex'=4,'ft'=8] {'ex'}, dimensions={0}, use_global_device_ids=true | all-gather | bytes 327680 | tf_op jit(solution)/shard_map/all_gather | solution.py:53
  31.2 11.2 %while.22 = (s32[]{:T(128)}, f32[32,2,128]{2,1,0:T(2,128)}, s32[]{:T(128)}, s32[96]{0:T(128)}, s32[]{:T(128)}, /*index=5*/s32[96]{0:T(128)}, bf16[32,2,128]{2,1,...) while((s32[]{:T(128)}, f32[32,2,128]{2,1,0:T(2,128)}, ...), condition=%wide.region_2.3_spmd.clone, body=%wide.region_0.2_spmd.clone.sunk | while | flops 1057926 | bytes 619155 | solution.py:34
  31.2 0.7 compare_select_fusion.8
  32.5 0.7 fusion.24
  33.2 1.4 convolution_select_fusion.4
  34.6 2.2 %scatter_fusion = f32[32,2,128]{2,1,0:T(2,128)} fusion(f32[32,2,128]{2,1,0:T(2,128)} %get-tuple-element.298, s32[16]{0:T(128)S(1)} %get-tuple-element.273, f32[16,2,128]{2,1,0:T(2,128)S(1)} %convolution_select_fusion.4), kind=kCustom, calls=%fused_computation.4.clone.clone.1 | custom fusion | flops 4096 | bytes 49216 | tf_op jit(solution)/shard_map/while/body/scatter-add | solution.py:32
  36.8 0.7 compare_select_fusion.8
  38.8 1.4 convolution_select_fusion.4
  40.2 2.2 %scatter_fusion = f32[32,2,128]{2,1,0:T(2,128)} fusion(f32[32,2,128]{2,1,0:T(2,128)} %get-tuple-element.298, s32[16]{0:T(128)S(1)} %get-tuple-element.273, f32[16,2,128]{2,1,0:T(2,128)S(1)} %convolution_select_fusion.4), kind=kCustom, calls=%fused_computation.4.clone.clone.1 | custom fusion | flops 4096 | bytes 49216 | tf_op jit(solution)/shard_map/while/body/scatter-add | solution.py:32
  42.4 8.9 %all-to-all-start.1 = ((f32[8,4,2,128]{3,2,1,0:T(2,128)}), f32[8,4,2,128]{3,2,1,0:T(2,128)S(1)}, u32[]{:S(2)}, u32[]{:S(2)}) async-start(f32[8,4,2,128]{3,2,1,0:T(2,128)} %bitcast.6), calls=%async_computation.1 | async-start | bytes 65536 | tf_op jit(solution)/shard_map/all_to_all | solution.py:61
  51.9 0.7 reduce.3
  52.7 3.4 %all-to-all-done.1 = f32[8,4,2,128]{3,2,1,0:T(2,128)S(1)} async-done(((f32[8,4,2,128]{3,2,1,0:T(2,128)}), f32[8,4,2,128]{3,2,1,0:T(2,128)S(1)}, u32[]{:S(2)}, u32[]{:S(2)}) %all-to-all-start.1) | async-done | bytes 32800 | tf_op jit(solution)/shard_map/all_to_all | solution.py:61
  56.2 1.7 %scatter_fusion.2 = f32[8,2,128]{2,1,0:T(2,128)S(1)} fusion(f32[8,2,128]{2,1,0:T(2,128)S(1)} %broadcast_in_dim.39, s32[32]{0:T(128)S(1)} %fusion.13, f32[32,2,128]{2,1,0:T(2,128)S(1)} %bitcast.27), kind=kCustom, calls=%fused_computation.6 | custom fusion | flops 8192 | bytes 98432 | tf_op jit(solution)/shard_map/scatter-add | solution.py:66
  57.9 1.2 gather_fusion.3
  59.1 3.3 %all-to-all-start.2 = ((bf16[8,4,2,128]{3,2,1,0:T(2,128)(2,1)}), bf16[8,4,2,128]{3,2,1,0:T(2,128)(2,1)S(1)}, u32[]{:S(2)}, u32[]{:S(2)}) async-start(bf16[8,4,2,128]{3,2,1,0:T(2,128)(2,1)} %bitcast.8), calls=%async_computation.2 | async-start | bytes 32768 | tf_op jit(solution)/shard_map/all_to_all | solution.py:70
  62.5 4.6 %all-to-all-done.2 = bf16[8,4,2,128]{3,2,1,0:T(2,128)(2,1)S(1)} async-done(((bf16[8,4,2,128]{3,2,1,0:T(2,128)(2,1)}), bf16[8,4,2,128]{3,2,1,0:T(2,128)(2,1)S(1)}, u32[]{:S(2)}, u32[]{:S(2)}) %all-to-all-start.2) | async-done | bytes 16416 | tf_op jit(solution)/shard_map/all_to_all | solution.py:70
  67.1 8.9 %while.23 = (s32[]{:T(128)}, f32[32,2,128]{2,1,0:T(2,128)S(1)}, s32[]{:T(128)}, s32[96]{0:T(128)}, s32[]{:T(128)}, /*index=5*/s32[96]{0:T(128)}, bf16[32,2,128]{...) while((s32[]{:T(128)}, f32[32,2,128]{2,1,0:T(2,128)S(1)}, ...), condition=%wide.region_6.7_spmd.clone, body=%wide.region_4.6_spmd.clone.sunk | while | flops 1057926 | bytes 619155 | solution.py:34
  67.1 0.8 compare_select_fusion.9
  68.5 0.7 fusion.27
  69.1 1.3 convolution_select_fusion.5
  70.4 1.1 scatter_fusion.1
  71.6 0.8 compare_select_fusion.9
  73.6 1.3 convolution_select_fusion.5
  74.9 1.1 scatter_fusion.1
  76.1 1.6 %scatter_fusion.3 = f32[512,2,128]{2,1,0:T(2,128)S(1)} fusion(f32[512,2,128]{2,1,0:T(2,128)S(1)} %broadcast_in_dim.38, s32[32]{0:T(128)S(1)} %fusion.12, f32[32,2,128]{2,1,0:T(2,128)S(1)} %get-tuple-element.102), kind=kCustom, calls=%fused_computation.7 | custom fusion | flops 8192 | bytes 98432 | tf_op jit(solution)/shard_map/scatter-add | solution.py:78
  77.8 0.8 copy-done
  79.9 70.7 %all-reduce.3.cloned.1.call-done = f32[512,2,128]{2,1,0:T(2,128)} async-done(((f32[512,2,128]{2,1,0:T(2,128)}), f32[512,2,128]{2,1,0:T(2,128)}) %all-reduce.3.cloned.1.call-update) | async-done | bytes 524304
  150.6 1.6 %fusion.11 = f32[128,1,2,128]{3,2,1,0:T(2,128)} fusion(f32[512,2,128]{2,1,0:T(2,128)} %all-reduce.3.cloned.1.call-done, u32[]{:T(128)S(6)} %multiply.1, f32[128,1,2,128]{3,2,1,0:T(2,128)S(1)} %copy-done.1), kind=kLoop, calls=%fused_computation.28 | loop fusion | flops 65536 | bytes 393220 | tf_op jit(solution)/shard_map/reshape | solution.py:82
  (36 shorter events, 6.6 us)
Async XLA Ops:
  6.5 51.3 %copy-start.2 = (f32[8,1,128]{2,1,0:T(1,128)S(1)}, f32[8,1,128]{2,1,0:T(1,128)}, u32[]{:S(2)}) copy-start(f32[8,1,128]{2,1,0:T(1,128)} %param.18) | copy-start | bytes 12292
  7.9 34.5 %all-to-all-start = ((s32[8,1,4]{2,1,0:T(1,128)}), s32[8,1,4]{2,1,0:T(1,128)S(1)}, u32[]{:S(2)}, u32[]{:S(2)}) async-start(s32[8,1,4]{2,1,0:T(1,128)} %copy.11), calls=%async_computation | async-start | bytes 8192 | tf_op jit(solution)/shard_map/all_to_all | solution.py:59
  42.4 36.2 %copy-start.3 = (u32[32]{0:T(128)S(1)}, u32[32]{0:T(128)}, u32[]{:S(2)}) copy-start(u32[32]{0:T(128)} %constant.68) | copy-start | bytes 388
  42.4 108.2 %copy-start.1 = (f32[128,1,2,128]{3,2,1,0:T(2,128)S(1)}, f32[128,1,2,128]{3,2,1,0:T(2,128)}, u32[]{:S(2)}) copy-start(f32[128,1,2,128]{3,2,1,0:T(2,128)} %param.19) | copy-start | bytes 393220
  42.4 13.8 %all-to-all-start.1 = ((f32[8,4,2,128]{3,2,1,0:T(2,128)}), f32[8,4,2,128]{3,2,1,0:T(2,128)S(1)}, u32[]{:S(2)}, u32[]{:S(2)}) async-start(f32[8,4,2,128]{3,2,1,0:T(2,128)} %bitcast.6), calls=%async_computation.1 | async-start | bytes 65536 | tf_op jit(solution)/shard_map/all_to_all | solution.py:61
  59.1 8.0 %all-to-all-start.2 = ((bf16[8,4,2,128]{3,2,1,0:T(2,128)(2,1)}), bf16[8,4,2,128]{3,2,1,0:T(2,128)(2,1)S(1)}, u32[]{:S(2)}, u32[]{:S(2)}) async-start(bf16[8,4,2,128]{3,2,1,0:T(2,128)(2,1)} %bitcast.8), calls=%async_computation.2 | async-start | bytes 32768 | tf_op jit(solution)/shard_map/all_to_all | solution.py:70
  62.4 88.2 %all-reduce.3.cloned.1.call-start = ((), (), s32[]{:S(2)}) async-start(), calls=%async_computation.3 | async-start | bytes 1048576
  77.8 0.8 copy-start
Sparse Core Ops, SparseCore 0:
  78.7 71.8 all-reduce.2
where the time goes:
time: 159 us
  waiting for transfers between devices  78.8 us (50%)
  other arithmetic  18.9 us (12%)
  starting transfers between devices  17.5 us (11%)
  between operations  14.8 us (9%)
  blocking collectives  14.3 us (9%)
  local copies, waits for them, and re-layouts  9.27 us (6%)
  matrix products  5.39 us (3%)
    unnamed x2, waiting for transfers between devices  70.7 us
    all_gather x1, blocking collectives, local(): whole_group = lax.all_gather(own_bf, 'ex', axis=0, tiled=True)  14.3 us
    all_to_all x1, starting transfers between devices, local(): lax.all_to_all(pieces, 'ft', split_axis=0, concat_axis=0, tiled=True)  8.91 us
    scatter-add x4, other arithmetic, advance(): return running.at[put_slots].add(result)  6.62 us
    all_to_all x1, starting transfers between devices, local(): lax.all_to_all(rows_listed, 'ft', split_axis=0, concat_axis=0, tiled=True)  5.2 us
    all_to_all x1, waiting for transfers between devices, local(): lax.all_to_all(reply, 'ft', split_axis=0, concat_axis=0, tiled=True)  4.64 us
    all_to_all x1, waiting for transfers between devices, local(): lax.all_to_all(pieces, 'ft', split_axis=0, concat_axis=0, tiled=True)  3.45 us
    all_to_all x1, starting transfers between devices, local(): lax.all_to_all(reply, 'ft', split_axis=0, concat_axis=0, tiled=True)  3.34 us
  transfers between devices with their start and end apart: 4, of which 3 were waited for; matrix products, arithmetic and copies ran while one was open for 10% of the time, Pallas kernels for 0%

commit v1 on v0

v1 whole, which is shorter than its diff:
```python
import functools
import jax
import jax.numpy as jnp
from jax import lax
from jax.experimental import pallas as pl
from jax.experimental.pallas import tpu as pltpu
from jax.sharding import PartitionSpec as P

scale_back = 4.0
tile_batch = 8


def exchange(axis, n, me, out_ref, in_ref, send_sem, recv_sem):
    copies = []
    for d in range(1, n):
        copy = pltpu.make_async_remote_copy(
            src_ref=out_ref.at[lax.rem(me + d, n)],
            dst_ref=in_ref.at[me],
            send_sem=send_sem.at[d],
            recv_sem=recv_sem.at[d],
            device_id={axis: lax.rem(me + d, n)},
            device_id_type=pl.DeviceIdType.MESH,
        )
        copy.start()
        copies.append(copy)
    return copies


def split_three(x):
    high = x.astype(jnp.bfloat16)
    rest = x - high.astype(jnp.float32)
    middle = rest.astype(jnp.bfloat16)
    low = (rest - middle.astype(jnp.float32)).astype(jnp.bfloat16)
    return jnp.concatenate([high, middle, low], axis=0)


def kernel(
    n_ex, n_ft, num_vecs,
    count_ref, cslot_ref, rslot_ref, need_ref, fold_ref, weight_ref, tiles_hbm, dir_hbm,
    out_ref,
    tiles_v, dir_v, need_out, need_in, fold_out, fold_in, vec_out, vec_in,
    mar_out, mar_in, sc_out, sc_in, cur_out, cur_in,
    col_f, row_f, spread, collect, place, local_sem, *sems,
):
    f32, bf16, i32 = jnp.float32, jnp.bfloat16, jnp.int32
    ex_me, ft_me = lax.axis_index("ex"), lax.axis_index("ft")
    asks, slots = need_ref.shape[2], fold_ref.shape[2]
    row_blocks = weight_ref.shape[0]
    slot_count, side = tiles_v.shape[0], tiles_v.shape[1]
    ask_rows, slot_rows = num_vecs * asks, num_vecs * slots
    all_asks, all_slots = n_ex * ask_rows, n_ft * slot_rows

    dir_copy = pltpu.make_async_copy(dir_hbm, dir_v, local_sem.at[0])
    dir_copy.start()
    tile_copy = pltpu.make_async_copy(tiles_hbm, tiles_v, local_sem.at[1])
    tile_copy.start()

    barrier = pltpu.get_barrier_semaphore()
    for d in range(1, n_ex):
        pl.semaphore_signal(barrier, inc=1, device_id={"ex": lax.rem(ex_me + d, n_ex)},
                            device_id_type=pl.DeviceIdType.MESH)
    for d in range(1, n_ft):
        pl.semaphore_signal(barrier, inc=1, device_id={"ft": lax.rem(ft_me + d, n_ft)},
                            device_id_type=pl.DeviceIdType.MESH)

    sub = lax.broadcasted_iota(i32, (asks, side), 0)
    for o in range(n_ex):
        block = jnp.zeros((asks, side), i32)
        for j in range(asks):
            block = jnp.where(sub == j, need_ref[0, o, j], block)
        need_out[o] = block
    sub = lax.broadcasted_iota(i32, (slot_rows, side), 0)
    for q in range(n_ft):
        block = jnp.zeros((slot_rows, side), i32)
        for i in range(slots):
            block = jnp.where(sub % slots == i, fold_ref[0, q, i], block)
        fold_out[q] = block + (sub // slots) * row_blocks

    pl.semaphore_wait(barrier, n_ex - 1 + n_ft - 1)

    need_copies = exchange("ex", n_ex, ex_me, need_out, need_in, sems[0], sems[1])
    fold_copies = exchange("ft", n_ft, ft_me, fold_out, fold_in, sems[2], sems[3])
    need_in[ex_me] = need_out[ex_me]
    fold_in[ft_me] = fold_out[ft_me]

    dir_copy.wait()
    dir_bf = dir_v[...].astype(bf16)
    col_rows = dir_v.shape[0]
    for copy in need_copies:
        copy.wait()
    asked = need_in[...]
    asked = jnp.concatenate([asked * num_vecs + k for k in range(num_vecs)], axis=1)
    asked = asked.reshape(all_asks, side)
    lane = lax.broadcasted_iota(i32, (all_asks, side), 1)
    hot = jnp.concatenate(
        [jnp.where(lane + base == asked, 1.0, 0.0) for base in range(0, col_rows, side)], axis=1
    )
    picked = jnp.dot(hot.astype(bf16), dir_bf, preferred_element_type=f32)
    vec_out[...] = picked.astype(bf16).reshape(vec_out.shape)
    vec_copies = exchange("ex", n_ex, ex_me, vec_out, vec_in, sems[4], sems[5])
    vec_in[ex_me] = vec_out[ex_me]

    spread[...] = hot.T.astype(bf16)
    for copy in fold_copies:
        copy.wait()
    lane = lax.broadcasted_iota(i32, (all_slots, side), 1)
    rows_hot = jnp.where(fold_in[...].reshape(all_slots, side) == lane, 1.0, 0.0)
    place[...] = rows_hot.astype(bf16)
    collect[...] = rows_hot.T[: num_vecs * row_blocks].astype(bf16)
    weight = jnp.concatenate([weight_ref[...]] * num_vecs, axis=0)

    for copy in vec_copies:
        copy.wait()
    col_f[...] = vec_in[...].reshape(all_asks, side).astype(f32)
    tile_copy.wait()

    live = count_ref[0]
    row_id = lax.broadcasted_iota(i32, (all_slots, side), 0)
    row_slot = (row_id // slot_rows) * slots + row_id % slots
    half = lax.broadcasted_iota(i32, (slot_rows, side), 0) // slots

    def forward(step, total):
        lefts, rights = [], []
        for u in range(tile_batch):
            t = step * tile_batch + u
            c, r = cslot_ref[t], rslot_ref[t]
            r = jnp.where(t < live, r, -1)
            base = (c // asks) * ask_rows + c % asks
            value = jnp.broadcast_to(col_f[pl.ds(base, 1), :], (slot_rows, side))
            for k in range(1, num_vecs):
                other = jnp.broadcast_to(col_f[pl.ds(base + k * asks, 1), :], (slot_rows, side))
                value = jnp.where(half >= k, other, value)
            value = jnp.concatenate([value] * n_ft, axis=0)
            lefts.append(jnp.where(row_slot == r, value, 0.0).astype(bf16))
            rights.append(tiles_v[t])
        return total + lax.dot_general(
            jnp.concatenate(lefts, axis=1), jnp.concatenate(rights, axis=1),
            (((1,), (1,)), ((), ())), preferred_element_type=f32,
        )

    part = lax.fori_loop(0, slot_count // tile_batch, forward, jnp.zeros((all_slots, side), f32))
    mar_out[...] = part.reshape(mar_out.shape)
    mar_copies = exchange("ft", n_ft, ft_me, mar_out, mar_in, sems[6], sems[7])
    mar_in[ft_me] = mar_out[ft_me]
    for copy in mar_copies:
        copy.wait()
    pieces = split_three(mar_in[...].reshape(all_slots, side))
    gather = collect[...]
    margins = jnp.dot(
        jnp.concatenate([gather] * 3, axis=1), pieces, preferred_element_type=f32
    )
    scaled = weight * margins
    filler = jnp.zeros((side - num_vecs * row_blocks, side), f32)
    scaled = jnp.concatenate([scaled, filler], axis=0).astype(bf16)
    answer = jnp.dot(place[...], scaled, preferred_element_type=f32)
    sc_out[...] = answer.astype(sc_out.dtype).reshape(sc_out.shape)
    sc_copies = exchange("ft", n_ft, ft_me, sc_out, sc_in, sems[8], sems[9])
    sc_in[ft_me] = sc_out[ft_me]
    for copy in sc_copies:
        copy.wait()
    row_f[...] = sc_in[...].astype(f32).reshape(all_slots, side)

    col_id = lax.broadcasted_iota(i32, (all_asks, side), 0)
    col_slot = (col_id // ask_rows) * asks + col_id % asks

    def backward(step, total):
        lefts, rights = [], []
        for u in range(tile_batch):
            t = step * tile_batch + u
            c, r = cslot_ref[t], rslot_ref[t]
            c = jnp.where(t < live, c, -1)
            base = (r // slots) * slot_rows + r % slots
            values = [
                jnp.broadcast_to(row_f[pl.ds(base + k * slots, 1), :], (asks, side))
                for k in range(num_vecs)
            ]
            value = jnp.concatenate(values * n_ex, axis=0)
            lefts.append(jnp.where(col_slot == c, value, 0.0).astype(bf16))
            rights.append(tiles_v[t])
        return total + jnp.dot(
            jnp.concatenate(lefts, axis=1), jnp.concatenate(rights, axis=0),
            preferred_element_type=f32,
        )

    part = lax.fori_loop(0, slot_count // tile_batch, backward, jnp.zeros((all_asks, side), f32))
    cur_out[...] = part.reshape(cur_out.shape)
    cur_copies = exchange("ex", n_ex, ex_me, cur_out, cur_in, sems[10], sems[11])
    cur_in[ex_me] = cur_out[ex_me]
    for copy in cur_copies:
        copy.wait()
    pieces = split_three(cur_in[...].reshape(all_asks, side))
    scatter = spread[...]
    curvature = jnp.dot(
        jnp.concatenate([scatter] * 3, axis=1), pieces, preferred_element_type=f32
    )
    out_ref[...] = dir_v[...] + scale_back * curvature


def local(tiles, tile_count, tile_cslot, tile_rslot, need_cols, fold_rows, weights, directions):
    n_ex, n_ft = lax.axis_size("ex"), lax.axis_size("ft")
    side = tiles.shape[1]
    col_blocks, num_vecs = directions.shape[0], directions.shape[2]
    row_blocks = weights.shape[0]
    asks, slots = need_cols.shape[2], fold_rows.shape[2]
    ask_rows, slot_rows = num_vecs * asks, num_vecs * slots
    f32, bf16, i32 = jnp.float32, jnp.bfloat16, jnp.int32
    smem = pl.BlockSpec(memory_space=pltpu.SMEM)
    vmem = pl.BlockSpec(memory_space=pltpu.VMEM)
    hbm = pl.BlockSpec(memory_space=pl.ANY)
    pairs = [n_ex, n_ft, n_ex, n_ft, n_ft, n_ex]
    out = pl.pallas_call(
        functools.partial(kernel, n_ex, n_ft, num_vecs),
        out_shape=jax.ShapeDtypeStruct((col_blocks * num_vecs, side), f32),
        in_specs=[smem] * 5 + [vmem, hbm, hbm],
        out_specs=vmem,
        scratch_shapes=[
            pltpu.VMEM(tiles.shape, bf16),
            pltpu.VMEM((col_blocks * num_vecs, side), f32),
            pltpu.VMEM((n_ex, asks, side), i32),
            pltpu.VMEM((n_ex, asks, side), i32),
            pltpu.VMEM((n_ft, slot_rows, side), i32),
            pltpu.VMEM((n_ft, slot_rows, side), i32),
            pltpu.VMEM((n_ex, ask_rows, side), bf16),
            pltpu.VMEM((n_ex, ask_rows, side), bf16),
            pltpu.VMEM((n_ft, slot_rows, side), f32),
            pltpu.VMEM((n_ft, slot_rows, side), f32),
            pltpu.VMEM((n_ft, slot_rows, side), f32),
            pltpu.VMEM((n_ft, slot_rows, side), f32),
            pltpu.VMEM((n_ex, ask_rows, side), f32),
            pltpu.VMEM((n_ex, ask_rows, side), f32),
            pltpu.VMEM((n_ex * ask_rows, side), f32),
            pltpu.VMEM((n_ft * slot_rows, side), f32),
            pltpu.VMEM((col_blocks * num_vecs, n_ex * ask_rows), bf16),
            pltpu.VMEM((num_vecs * row_blocks, n_ft * slot_rows), bf16),
            pltpu.VMEM((n_ft * slot_rows, side), bf16),
            pltpu.SemaphoreType.DMA((2,)),
        ] + [pltpu.SemaphoreType.DMA((n,)) for n in pairs for _ in range(2)],
        compiler_params=pltpu.CompilerParams(collective_id=0, has_side_effects=True),
    )(
        tile_count, tile_cslot, tile_rslot, need_cols, fold_rows,
        weights.reshape(row_blocks, side), tiles,
        directions.reshape(col_blocks * num_vecs, side),
    )
    return out.reshape(directions.shape)


def solution(mesh):
    return jax.shard_map(
        local,
        mesh=mesh,
        in_specs=(
            P(("ex", "ft"), None, None),
            P(("ex", "ft")),
            P(("ex", "ft")),
            P(("ex", "ft")),
            P(("ex", "ft"), None, None),
            P(("ex", "ft"), None, None),
            P("ft", "ex", None),
            P("ex", "ft", None, None),
        ),
        out_specs=P("ex", "ft", None, None),
        check_vma=False,
    )
```

time: 159 us -> 33.9 us (0.21)
  waiting for transfers between devices: 78.8 us -> 0 us
  Pallas kernels: 0 us -> 30.1 us
  other arithmetic: 18.9 us -> 0 us
  starting transfers between devices: 17.5 us -> 0 us
  blocking collectives: 14.3 us -> 0 us
  between operations: 14.8 us -> 0.66 us
  local copies, waits for them, and re-layouts: 9.27 us -> 2.92 us
  matrix products: 5.39 us -> 0 us
    unnamed x2 -> x0, waiting for transfers between devices: 70.7 us -> none
    pallas_call x0 -> x1, Pallas kernels: none -> 30.1 us  [local(): pl.pallas_call(functools.partial(kernel, n_ex, n_ft, num_vecs), out_shape...]
    all_to_all x3 -> x0, starting transfers between devices: 17.4 us -> none  [the longest x1 8.91 us: local(): lax.all_to_all(pieces, 'ft', split_axis=0, concat_axis=0, tiled=True)]
    all_gather x1 -> x0, blocking collectives: 14.3 us -> none  [local(): whole_group = lax.all_gather(own_bf, 'ex', axis=0, tiled=True)]
    scatter-add x6 -> x0, other arithmetic: 9.94 us -> none  [the longest x4 6.62 us: advance(): return running.at[put_slots].add(result)]
    all_to_all x3 -> x0, waiting for transfers between devices: 8.08 us -> none  [the longest x1 4.64 us: local(): lax.all_to_all(reply, 'ft', split_axis=0, concat_axis=0, tiled=True)]
    dot_general x4 -> x0, matrix products: 5.39 us -> none  [the longest x2 2.81 us: advance(): jnp.einsum('tij,tkj->tki', tile_group, inputs, preferred_element_type=jnp...]
    gather x6 -> x0, local copies, waits for them, and re-layouts: 4.15 us -> none  [the longest x4 2.35 us: advance(): inputs = source[pick_slots]]
  transfers between devices with their start and end apart: 4 -> 0, of which waited for: 3 -> 0; matrix products, arithmetic and copies ran while one was open for 10% -> 0% of each run, Pallas kernels for 0% -> 0%
where the time goes in v1:
time: 33.9 us; the launch traced here: 33.7 us
  Pallas kernels  30.1 us (89%)
  local copies, waits for them, and re-layouts  2.92 us (9%)
  between operations  0.66 us (2%)
    pallas_call x1, Pallas kernels, local(): pl.pallas_call(functools.partial(kernel, n_ex, n_ft, num_vecs), out_shape...  30.1 us
    unnamed x2, local copies, waits for them, and re-layouts  2.92 us

profile of v1, /device:TPU:0, one launch (start us, length us, event | category | flops | bytes accessed | tf_op | source)
XLA Modules:
  0.0 33.7 jit_solution(13955839160210648814)
XLA Ops:
  0.7 1.3 %copy.9.fold_ref = s32[1,8,4]{2,1,0:T(8,128)} copy(s32[1,8,4]{1,2,0:T(4,128)} %param.13) | data formatting | bytes 256 | tf_op args[5]
  2.0 30.1 %shard_map.82 = f32[256,128]{1,0:T(8,128)} custom-call(s32[1]{0:T(128)S(6)} %copy.12.count_ref, s32[96]{0:T(128)} %cslot_ref.1, s32[96]{0:T(128)} %rslot_ref.1, s32[1,4,8]{2,1,0:T(4,128)} %need_ref.1, s32[1,8,4]{2,1,0:T(8,128)} %copy.9.fold_ref, f32[8,128]{1,0:T(8,128)} %bitcast.7, bf16[96,128,128]{2,1,0:T(8,128)(2,1)} %tiles_hbm.1, f32[256,128]{1,0:T(8,128)} %bitcast.6), custom_call_target="tpu_custom_call" | custom-call | tf_op jit(solution)/shard_map/pallas_call | solution.py:211
  32.1 1.6 %copy.13 = f32[128,1,2,128]{3,2,1,0:T(2,128)} copy(f32[128,1,2,128]{3,2,1,0:T(2,128)} %bitcast.5) | data formatting | bytes 262144

commit v2 on v1

--- a/solution.py
+++ b/solution.py
@@ -10,15 +10,27 @@
 tile_batch = 8
 
 
+def partner(me, d, n):
+    if n & (n - 1):
+        return lax.rem(me + d, n)
+    other, bit = me, 1
+    while bit < n:
+        if d & bit:
+            other = other + bit * (1 - 2 * (me // bit % 2))
+        bit *= 2
+    return other
+
+
 def exchange(axis, n, me, out_ref, in_ref, send_sem, recv_sem):
     copies = []
-    for d in range(1, n):
+    for d in range(n - 1, 0, -1):
+        peer = partner(me, d, n)
         copy = pltpu.make_async_remote_copy(
-            src_ref=out_ref.at[lax.rem(me + d, n)],
+            src_ref=out_ref.at[peer],
             dst_ref=in_ref.at[me],
             send_sem=send_sem.at[d],
             recv_sem=recv_sem.at[d],
-            device_id={axis: lax.rem(me + d, n)},
+            device_id={axis: peer},
             device_id_type=pl.DeviceIdType.MESH,
         )
         copy.start()
@@ -36,52 +48,71 @@
 
 def kernel(
     n_ex, n_ft, num_vecs,
-    count_ref, cslot_ref, rslot_ref, need_ref, fold_ref, weight_ref, tiles_hbm, dir_hbm,
+    count_ref, cslot_hbm, rslot_hbm, need_hbm, fold_hbm, weight_hbm, tiles_hbm, dir_hbm,
     out_ref,
+    cslot_ref, rslot_ref, need_ref, fold_ref, weight_ref,
+    col_base, row_base, col_live, row_live,
     tiles_v, dir_v, need_out, need_in, fold_out, fold_in, vec_out, vec_in,
     mar_out, mar_in, sc_out, sc_in, cur_out, cur_in,
     col_f, row_f, spread, collect, place, local_sem, *sems,
 ):
     f32, bf16, i32 = jnp.float32, jnp.bfloat16, jnp.int32
     ex_me, ft_me = lax.axis_index("ex"), lax.axis_index("ft")
-    asks, slots = need_ref.shape[2], fold_ref.shape[2]
+    asks, slots = need_ref.shape[2], fold_ref.shape[1]
     row_blocks = weight_ref.shape[0]
     slot_count, side = tiles_v.shape[0], tiles_v.shape[1]
     ask_rows, slot_rows = num_vecs * asks, num_vecs * slots
     all_asks, all_slots = n_ex * ask_rows, n_ft * slot_rows
 
-    dir_copy = pltpu.make_async_copy(dir_hbm, dir_v, local_sem.at[0])
-    dir_copy.start()
-    tile_copy = pltpu.make_async_copy(tiles_hbm, tiles_v, local_sem.at[1])
-    tile_copy.start()
-
     barrier = pltpu.get_barrier_semaphore()
-    for d in range(1, n_ex):
-        pl.semaphore_signal(barrier, inc=1, device_id={"ex": lax.rem(ex_me + d, n_ex)},
-                            device_id_type=pl.DeviceIdType.MESH)
-    for d in range(1, n_ft):
-        pl.semaphore_signal(barrier, inc=1, device_id={"ft": lax.rem(ft_me + d, n_ft)},
-                            device_id_type=pl.DeviceIdType.MESH)
-
+    for axis, n, me in (("ex", n_ex, ex_me), ("ft", n_ft, ft_me)):
+        for d in range(n - 1, 0, -1):
+            pl.semaphore_signal(barrier, inc=1, device_id={axis: partner(me, d, n)},
+                                device_id_type=pl.DeviceIdType.MESH)
+
+    fetched = []
+    for index, (source, target) in enumerate((
+        (need_hbm, need_ref), (fold_hbm, fold_ref),
+        (cslot_hbm, cslot_ref), (rslot_hbm, rslot_ref), (dir_hbm, dir_v),
+        (weight_hbm, weight_ref), (tiles_hbm, tiles_v),
+    )):
+        fetched.append(pltpu.make_async_copy(source, target, local_sem.at[index]))
+        fetched[-1].start()
+    need_copy, fold_copy, cslot_copy, rslot_copy, dir_copy, weight_copy, tile_copy = fetched
+
+    need_copy.wait()
     sub = lax.broadcasted_iota(i32, (asks, side), 0)
     for o in range(n_ex):
         block = jnp.zeros((asks, side), i32)
         for j in range(asks):
             block = jnp.where(sub == j, need_ref[0, o, j], block)
         need_out[o] = block
+    pl.semaphore_wait(barrier, n_ex - 1 + n_ft - 1)
+
+    need_copies = exchange("ex", n_ex, ex_me, need_out, need_in, sems[0], sems[1])
+    need_in[ex_me] = need_out[ex_me]
+
+    fold_copy.wait()
     sub = lax.broadcasted_iota(i32, (slot_rows, side), 0)
     for q in range(n_ft):
         block = jnp.zeros((slot_rows, side), i32)
         for i in range(slots):
-            block = jnp.where(sub % slots == i, fold_ref[0, q, i], block)
+            block = jnp.where(sub % slots == i, fold_ref[0, i, q], block)
         fold_out[q] = block + (sub // slots) * row_blocks
 
-    pl.semaphore_wait(barrier, n_ex - 1 + n_ft - 1)
-
-    need_copies = exchange("ex", n_ex, ex_me, need_out, need_in, sems[0], sems[1])
-    fold_copies = exchange("ft", n_ft, ft_me, fold_out, fold_in, sems[2], sems[3])
-    need_in[ex_me] = need_out[ex_me]
-    fold_in[ft_me] = fold_out[ft_me]
+    cslot_copy.wait()
+    rslot_copy.wait()
+    live = count_ref[0]
+
+    @pl.loop(0, slot_count // tile_batch)
+    def _(step):
+        for u in range(tile_batch):
+            t = step * tile_batch + u
+            c, r = cslot_ref[t], rslot_ref[t]
+            col_base[t] = lax.div(c, asks) * ask_rows + lax.rem(c, asks)
+            row_base[t] = lax.div(r, slots) * slot_rows + lax.rem(r, slots)
+            col_live[t] = jnp.where(t < live, c, -1)
+            row_live[t] = jnp.where(t < live, r, -1)
 
     dir_copy.wait()
     dir_bf = dir_v[...].astype(bf16)
@@ -99,6 +130,8 @@
     vec_out[...] = picked.astype(bf16).reshape(vec_out.shape)
     vec_copies = exchange("ex", n_ex, ex_me, vec_out, vec_in, sems[4], sems[5])
     vec_in[ex_me] = vec_out[ex_me]
+    fold_copies = exchange("ft", n_ft, ft_me, fold_out, fold_in, sems[2], sems[3])
+    fold_in[ft_me] = fold_out[ft_me]
 
     spread[...] = hot.T.astype(bf16)
     for copy in fold_copies:
@@ -107,6 +140,7 @@
     rows_hot = jnp.where(fold_in[...].reshape(all_slots, side) == lane, 1.0, 0.0)
     place[...] = rows_hot.astype(bf16)
     collect[...] = rows_hot.T[: num_vecs * row_blocks].astype(bf16)
+    weight_copy.wait()
     weight = jnp.concatenate([weight_ref[...]] * num_vecs, axis=0)
 
     for copy in vec_copies:
@@ -114,7 +148,6 @@
     col_f[...] = vec_in[...].reshape(all_asks, side).astype(f32)
     tile_copy.wait()
 
-    live = count_ref[0]
     row_id = lax.broadcasted_iota(i32, (all_slots, side), 0)
     row_slot = (row_id // slot_rows) * slots + row_id % slots
     half = lax.broadcasted_iota(i32, (slot_rows, side), 0) // slots
@@ -123,9 +156,7 @@
         lefts, rights = [], []
         for u in range(tile_batch):
             t = step * tile_batch + u
-            c, r = cslot_ref[t], rslot_ref[t]
-            r = jnp.where(t < live, r, -1)
-            base = (c // asks) * ask_rows + c % asks
+            base, r = col_base[t], row_live[t]
             value = jnp.broadcast_to(col_f[pl.ds(base, 1), :], (slot_rows, side))
             for k in range(1, num_vecs):
                 other = jnp.broadcast_to(col_f[pl.ds(base + k * asks, 1), :], (slot_rows, side))
@@ -167,9 +198,7 @@
         lefts, rights = [], []
         for u in range(tile_batch):
             t = step * tile_batch + u
-            c, r = cslot_ref[t], rslot_ref[t]
-            c = jnp.where(t < live, c, -1)
-            base = (r // slots) * slot_rows + r % slots
+            base, c = row_base[t], col_live[t]
             values = [
                 jnp.broadcast_to(row_f[pl.ds(base + k * slots, 1), :], (asks, side))
                 for k in range(num_vecs)
@@ -193,7 +222,7 @@
     curvature = jnp.dot(
         jnp.concatenate([scatter] * 3, axis=1), pieces, preferred_element_type=f32
     )
-    out_ref[...] = dir_v[...] + scale_back * curvature
+    out_ref[...] = curvature
 
 
 def local(tiles, tile_count, tile_cslot, tile_rslot, need_cols, fold_rows, weights, directions):
@@ -204,16 +233,22 @@
     asks, slots = need_cols.shape[2], fold_rows.shape[2]
     ask_rows, slot_rows = num_vecs * asks, num_vecs * slots
     f32, bf16, i32 = jnp.float32, jnp.bfloat16, jnp.int32
-    smem = pl.BlockSpec(memory_space=pltpu.SMEM)
     vmem = pl.BlockSpec(memory_space=pltpu.VMEM)
-    hbm = pl.BlockSpec(memory_space=pl.ANY)
+    hbm = pl.BlockSpec(memory_space=pltpu.HBM)
     pairs = [n_ex, n_ft, n_ex, n_ft, n_ft, n_ex]
+    own = directions.reshape(col_blocks * num_vecs, side)
     out = pl.pallas_call(
         functools.partial(kernel, n_ex, n_ft, num_vecs),
         out_shape=jax.ShapeDtypeStruct((col_blocks * num_vecs, side), f32),
-        in_specs=[smem] * 5 + [vmem, hbm, hbm],
+        in_specs=[pl.BlockSpec(memory_space=pltpu.SMEM)] + [hbm] * 7,
         out_specs=vmem,
         scratch_shapes=[
+            pltpu.SMEM(tile_cslot.shape, i32),
+            pltpu.SMEM(tile_rslot.shape, i32),
+            pltpu.SMEM(need_cols.shape, i32),
+            pltpu.SMEM((1, slots, n_ft), i32),
+            pltpu.VMEM((row_blocks, side), f32),
+        ] + [pltpu.SMEM(tile_cslot.shape, i32)] * 4 + [
             pltpu.VMEM(tiles.shape, bf16),
             pltpu.VMEM((col_blocks * num_vecs, side), f32),
             pltpu.VMEM((n_ex, asks, side), i32),
@@ -233,15 +268,14 @@
             pltpu.VMEM((col_blocks * num_vecs, n_ex * ask_rows), bf16),
             pltpu.VMEM((num_vecs * row_blocks, n_ft * slot_rows), bf16),
             pltpu.VMEM((n_ft * slot_rows, side), bf16),
-            pltpu.SemaphoreType.DMA((2,)),
+            pltpu.SemaphoreType.DMA((7,)),
         ] + [pltpu.SemaphoreType.DMA((n,)) for n in pairs for _ in range(2)],
-        compiler_params=pltpu.CompilerParams(collective_id=0, has_side_effects=True),
-    )(
-        tile_count, tile_cslot, tile_rslot, need_cols, fold_rows,
-        weights.reshape(row_blocks, side), tiles,
-        directions.reshape(col_blocks * num_vecs, side),
-    )
-    return out.reshape(directions.shape)
+        compiler_params=pltpu.CompilerParams(collective_id=0, has_side_effects=True, vmem_limit_bytes=8 << 20),
+    )(tile_count, *(pltpu.with_memory_space_constraint(x, pltpu.HBM) for x in (
+        tile_cslot, tile_rslot, need_cols, fold_rows.transpose(0, 2, 1),
+        weights.reshape(row_blocks, side), tiles, own,
+    )))
+    return (own + scale_back * out).reshape(directions.shape)
 
 
 def solution(mesh):

time: 33.9 us -> 30.2 us (0.89)
  local copies, waits for them, and re-layouts: 2.92 us -> 0.01 us
  Pallas kernels: 30.1 us -> 28.6 us
  other arithmetic: 0 us -> 0.67 us
    unnamed x2, local copies, waits for them, and re-layouts: 2.92 us -> 0.01 us
    pallas_call x1, Pallas kernels: 30.1 us -> 28.6 us  [local(): pl.pallas_call(functools.partial(kernel, n_ex, n_ft, num_vecs), out_shape...]
    add x0 -> x1, other arithmetic: none -> 0.67 us  [local(): return (own + scale_back * out).reshape(directions.shape)]
where the time goes in v2:
time: 30.2 us; the launch traced here: 30 us
  Pallas kernels  28.6 us (95%)
  between operations  0.7 us (2%)
  other arithmetic  0.67 us (2%)
    pallas_call x1, Pallas kernels, local(): pl.pallas_call(functools.partial(kernel, n_ex, n_ft, num_vecs), out_shape...  28.6 us
    add x1, other arithmetic, local(): return (own + scale_back * out).reshape(directions.shape)  0.67 us

profile of v2, /device:TPU:0, one launch (start us, length us, event | category | flops | bytes accessed | tf_op | source)
XLA Modules:
  0.0 30.0 jit_solution(17290661264197907615)
XLA Ops:
  0.0 0.0 copy-start
  0.7 28.6 %shard_map.82 = f32[256,128]{1,0:T(8,128)S(1)} custom-call(s32[1]{0:T(128)S(6)} %copy.10.count_ref, s32[96]{0:T(128)} %cslot_hbm.1, s32[96]{0:T(128)} %rslot_hbm.1, s32[1,4,8]{2,1,0:T(4,128)} %need_hbm.1, s32[1,4,8]{2,1,0:T(4,128)} %bitcast.9, f32[8,128]{1,0:T(8,128)} %bitcast.8, bf16[96,128,128]{2,1,0:T(8,128)(2,1)} %tiles_hbm.1, f32[256,128]{1,0:T(8,128)} %bitcast.6), custom_call_target="tpu_custom_call" | custom-call | tf_op jit(solution)/shard_map/pallas_call | solution.py:240
  29.3 0.0 copy-done
  29.3 0.7 %multiply_add_fusion = f32[256,128]{1,0:T(8,128)} fusion(f32[256,128]{1,0:T(8,128)S(1)} %bitcast.7, f32[256,128]{1,0:T(8,128)S(1)} %shard_map.82), kind=kLoop, calls=%fused_computation | loop fusion | flops 65536 | bytes 393216 | tf_op jit(solution)/shard_map/add | solution.py:278
Async XLA Ops:
  0.0 29.3 %copy-start = (f32[128,1,2,128]{3,2,1,0:T(2,128)S(1)}, f32[128,1,2,128]{3,2,1,0:T(2,128)}, u32[]{:S(2)}) copy-start(f32[128,1,2,128]{3,2,1,0:T(2,128)} %param.15) | copy-start | bytes 393220

commit v3 on v2

--- a/solution.py
+++ b/solution.py
@@ -7,7 +7,7 @@
 from jax.sharding import PartitionSpec as P
 
 scale_back = 4.0
-tile_batch = 8
+tile_batch = 32
 
 
 def partner(me, d, n):
@@ -21,12 +21,12 @@
     return other
 
 
-def exchange(axis, n, me, out_ref, in_ref, send_sem, recv_sem):
+def exchange(axis, n, me, out_ref, in_ref, send_sem, recv_sem, shared=False):
     copies = []
     for d in range(n - 1, 0, -1):
         peer = partner(me, d, n)
         copy = pltpu.make_async_remote_copy(
-            src_ref=out_ref.at[peer],
+            src_ref=out_ref if shared else out_ref.at[peer],
             dst_ref=in_ref.at[me],
             send_sem=send_sem.at[d],
             recv_sem=recv_sem.at[d],
@@ -43,7 +43,7 @@
     rest = x - high.astype(jnp.float32)
     middle = rest.astype(jnp.bfloat16)
     low = (rest - middle.astype(jnp.float32)).astype(jnp.bfloat16)
-    return jnp.concatenate([high, middle, low], axis=0)
+    return high, middle, low
 
 
 def kernel(
@@ -52,9 +52,9 @@
     out_ref,
     cslot_ref, rslot_ref, need_ref, fold_ref, weight_ref,
     col_base, row_base, col_live, row_live,
-    tiles_v, dir_v, need_out, need_in, fold_out, fold_in, vec_out, vec_in,
-    mar_out, mar_in, sc_out, sc_in, cur_out, cur_in,
-    col_f, row_f, spread, collect, place, local_sem, *sems,
+    tiles_v, dir_v, need_out, need_in, own_code, info_out, info_in, vec_out, vec_in,
+    mar_out, mar_in, cur_out, cur_in,
+    col_f, row_f, spread, collect, weight_own, local_sem, *sems,
 ):
     f32, bf16, i32 = jnp.float32, jnp.bfloat16, jnp.int32
     ex_me, ft_me = lax.axis_index("ex"), lax.axis_index("ft")
@@ -93,12 +93,21 @@
     need_in[ex_me] = need_out[ex_me]
 
     fold_copy.wait()
-    sub = lax.broadcasted_iota(i32, (slot_rows, side), 0)
+    weight_copy.wait()
+    width = own_code.shape[1]
+    sub = lax.broadcasted_iota(i32, (slot_rows, width), 0)
+    lane = lax.broadcasted_iota(i32, (8, width), 1) % all_slots
+    codes = (lane % slot_rows) // slots * n_ft * row_blocks + lane // slot_rows * row_blocks
+    lane_slot = lane // slot_rows * slots + lane % slots
+    listed = jnp.zeros((8, width), i32)
     for q in range(n_ft):
-        block = jnp.zeros((slot_rows, side), i32)
+        block = jnp.zeros((slot_rows, width), i32)
         for i in range(slots):
             block = jnp.where(sub % slots == i, fold_ref[0, i, q], block)
-        fold_out[q] = block + (sub // slots) * row_blocks
+            listed = jnp.where(lane_slot == q * slots + i, fold_ref[0, i, q], listed)
+        own_code[pl.ds(q * slot_rows, slot_rows), :] = block + q * row_blocks
+    info_out[pl.ds(0, row_blocks), pl.ds(0, side)] = weight_ref[...]
+    info_out[pl.ds(row_blocks, 8), :] = (listed + codes).astype(f32)
 
     cslot_copy.wait()
     rslot_copy.wait()
@@ -130,18 +139,32 @@
     vec_out[...] = picked.astype(bf16).reshape(vec_out.shape)
     vec_copies = exchange("ex", n_ex, ex_me, vec_out, vec_in, sems[4], sems[5])
     vec_in[ex_me] = vec_out[ex_me]
-    fold_copies = exchange("ft", n_ft, ft_me, fold_out, fold_in, sems[2], sems[3])
-    fold_in[ft_me] = fold_out[ft_me]
+    info_copies = exchange(
+        "ft", n_ft, ft_me, info_out, info_in, sems[2], sems[3], shared=True
+    )
+    info_in[ft_me] = info_out[...]
 
     spread[...] = hot.T.astype(bf16)
-    for copy in fold_copies:
-        copy.wait()
-    lane = lax.broadcasted_iota(i32, (all_slots, side), 1)
-    rows_hot = jnp.where(fold_in[...].reshape(all_slots, side) == lane, 1.0, 0.0)
-    place[...] = rows_hot.astype(bf16)
-    collect[...] = rows_hot.T[: num_vecs * row_blocks].astype(bf16)
-    weight_copy.wait()
-    weight = jnp.concatenate([weight_ref[...]] * num_vecs, axis=0)
+    for copy in info_copies:
+        copy.wait()
+    code = own_code[...]
+    row_total = n_ft * row_blocks
+    lane = lax.broadcasted_iota(i32, (all_slots, row_total), 1)
+    hot = jnp.where(code[:, :row_total] == lane, 1.0, 0.0).astype(bf16)
+    weights = info_in[:, pl.ds(0, row_blocks), pl.ds(0, side)].reshape(row_total, side)
+    weight_own[...] = sum(
+        jnp.dot(hot, piece, preferred_element_type=f32) for piece in split_three(weights)
+    )
+    sub = lax.broadcasted_iota(i32, (all_slots, width), 0) % slot_rows // slots
+    code = (code + sub * row_total).astype(f32)
+    group = width // all_slots
+    lane = lax.broadcasted_iota(i32, (1, width), 1) // all_slots
+    for g in range(n_ft // group):
+        line = info_in[g * group, pl.ds(row_blocks, 1), :]
+        for h in range(1, group):
+            other = info_in[g * group + h, pl.ds(row_blocks, 1), :]
+            line = jnp.where(lane == h, other, line)
+        collect[:, pl.ds(g * width, width)] = jnp.where(code == line, 1.0, 0.0).astype(bf16)
 
     for copy in vec_copies:
         copy.wait()
@@ -170,26 +193,15 @@
         )
 
     part = lax.fori_loop(0, slot_count // tile_batch, forward, jnp.zeros((all_slots, side), f32))
-    mar_out[...] = part.reshape(mar_out.shape)
-    mar_copies = exchange("ft", n_ft, ft_me, mar_out, mar_in, sems[6], sems[7])
-    mar_in[ft_me] = mar_out[ft_me]
+    mar_out[...] = part.astype(bf16)
+    mar_copies = exchange("ft", n_ft, ft_me, mar_out, mar_in, sems[6], sems[7], shared=True)
+    mar_in[ft_me] = mar_out[...]
     for copy in mar_copies:
         copy.wait()
-    pieces = split_three(mar_in[...].reshape(all_slots, side))
-    gather = collect[...]
     margins = jnp.dot(
-        jnp.concatenate([gather] * 3, axis=1), pieces, preferred_element_type=f32
-    )
-    scaled = weight * margins
-    filler = jnp.zeros((side - num_vecs * row_blocks, side), f32)
-    scaled = jnp.concatenate([scaled, filler], axis=0).astype(bf16)
-    answer = jnp.dot(place[...], scaled, preferred_element_type=f32)
-    sc_out[...] = answer.astype(sc_out.dtype).reshape(sc_out.shape)
-    sc_copies = exchange("ft", n_ft, ft_me, sc_out, sc_in, sems[8], sems[9])
-    sc_in[ft_me] = sc_out[ft_me]
-    for copy in sc_copies:
-        copy.wait()
-    row_f[...] = sc_in[...].astype(f32).reshape(all_slots, side)
+        collect[...], mar_in[...].reshape(n_ft * all_slots, side), preferred_element_type=f32
+    )
+    row_f[...] = (weight_own[...] * margins).astype(bf16).astype(f32)
 
     col_id = lax.broadcasted_iota(i32, (all_asks, side), 0)
     col_slot = (col_id // ask_rows) * asks + col_id % asks
@@ -213,11 +225,11 @@
 
     part = lax.fori_loop(0, slot_count // tile_batch, backward, jnp.zeros((all_asks, side), f32))
     cur_out[...] = part.reshape(cur_out.shape)
-    cur_copies = exchange("ex", n_ex, ex_me, cur_out, cur_in, sems[10], sems[11])
+    cur_copies = exchange("ex", n_ex, ex_me, cur_out, cur_in, sems[8], sems[9])
     cur_in[ex_me] = cur_out[ex_me]
     for copy in cur_copies:
         copy.wait()
-    pieces = split_three(cur_in[...].reshape(all_asks, side))
+    pieces = jnp.concatenate(split_three(cur_in[...].reshape(all_asks, side)), axis=0)
     scatter = spread[...]
     curvature = jnp.dot(
         jnp.concatenate([scatter] * 3, axis=1), pieces, preferred_element_type=f32
@@ -235,7 +247,9 @@
     f32, bf16, i32 = jnp.float32, jnp.bfloat16, jnp.int32
     vmem = pl.BlockSpec(memory_space=pltpu.VMEM)
     hbm = pl.BlockSpec(memory_space=pltpu.HBM)
-    pairs = [n_ex, n_ft, n_ex, n_ft, n_ft, n_ex]
+    pairs = [n_ex, n_ft, n_ex, n_ft, n_ex]
+    all_slots = n_ft * slot_rows
+    width = max(all_slots, 128)
     own = directions.reshape(col_blocks * num_vecs, side)
     out = pl.pallas_call(
         functools.partial(kernel, n_ex, n_ft, num_vecs),
@@ -253,24 +267,23 @@
             pltpu.VMEM((col_blocks * num_vecs, side), f32),
             pltpu.VMEM((n_ex, asks, side), i32),
             pltpu.VMEM((n_ex, asks, side), i32),
-            pltpu.VMEM((n_ft, slot_rows, side), i32),
-            pltpu.VMEM((n_ft, slot_rows, side), i32),
+            pltpu.VMEM((all_slots, width), i32),
+            pltpu.VMEM((row_blocks + 8, width), f32),
+            pltpu.VMEM((n_ft, row_blocks + 8, width), f32),
             pltpu.VMEM((n_ex, ask_rows, side), bf16),
             pltpu.VMEM((n_ex, ask_rows, side), bf16),
-            pltpu.VMEM((n_ft, slot_rows, side), f32),
-            pltpu.VMEM((n_ft, slot_rows, side), f32),
-            pltpu.VMEM((n_ft, slot_rows, side), f32),
-            pltpu.VMEM((n_ft, slot_rows, side), f32),
+            pltpu.VMEM((all_slots, side), bf16),
+            pltpu.VMEM((n_ft, all_slots, side), bf16),
             pltpu.VMEM((n_ex, ask_rows, side), f32),
             pltpu.VMEM((n_ex, ask_rows, side), f32),
             pltpu.VMEM((n_ex * ask_rows, side), f32),
             pltpu.VMEM((n_ft * slot_rows, side), f32),
             pltpu.VMEM((col_blocks * num_vecs, n_ex * ask_rows), bf16),
-            pltpu.VMEM((num_vecs * row_blocks, n_ft * slot_rows), bf16),
-            pltpu.VMEM((n_ft * slot_rows, side), bf16),
+            pltpu.VMEM((all_slots, n_ft * all_slots), bf16),
+            pltpu.VMEM((all_slots, side), f32),
             pltpu.SemaphoreType.DMA((7,)),
         ] + [pltpu.SemaphoreType.DMA((n,)) for n in pairs for _ in range(2)],
-        compiler_params=pltpu.CompilerParams(collective_id=0, has_side_effects=True, vmem_limit_bytes=8 << 20),
+        compiler_params=pltpu.CompilerParams(collective_id=0, has_side_effects=True, vmem_limit_bytes=24 << 20),
     )(tile_count, *(pltpu.with_memory_space_constraint(x, pltpu.HBM) for x in (
         tile_cslot, tile_rslot, need_cols, fold_rows.transpose(0, 2, 1),
         weights.reshape(row_blocks, side), tiles, own,

time: 30.2 us -> 24.5 us (0.81)
  Pallas kernels: 28.6 us -> 23 us
    pallas_call x1, Pallas kernels: 28.6 us -> 23 us  [local(): pl.pallas_call(functools.partial(kernel, n_ex, n_ft, num_vecs), out_shape...]
where the time goes in v3:
time: 24.5 us; the launch traced here: 24.4 us
  Pallas kernels  23 us (94%)
  between operations  0.7 us (3%)
  other arithmetic  0.67 us (3%)
    pallas_call x1, Pallas kernels, local(): pl.pallas_call(functools.partial(kernel, n_ex, n_ft, num_vecs), out_shape...  23 us
    add x1, other arithmetic, local(): return (own + scale_back * out).reshape(directions.shape)  0.67 us

profile of v3, /device:TPU:0, one launch (start us, length us, event | category | flops | bytes accessed | tf_op | source)
XLA Modules:
  0.0 24.4 jit_solution(14172862217674379921)
XLA Ops:
  0.0 0.0 copy-start
  0.7 23.0 %shard_map.82 = f32[256,128]{1,0:T(8,128)S(1)} custom-call(s32[1]{0:T(128)S(6)} %copy.10.count_ref, s32[96]{0:T(128)} %cslot_hbm.1, s32[96]{0:T(128)} %rslot_hbm.1, s32[1,4,8]{2,1,0:T(4,128)} %need_hbm.1, s32[1,4,8]{2,1,0:T(4,128)} %bitcast.9, f32[8,128]{1,0:T(8,128)} %bitcast.8, bf16[96,128,128]{2,1,0:T(8,128)(2,1)} %tiles_hbm.1, f32[256,128]{1,0:T(8,128)} %bitcast.6), custom_call_target="tpu_custom_call" | custom-call | tf_op jit(solution)/shard_map/pallas_call | solution.py:254
  23.7 0.0 copy-done
  23.7 0.7 %multiply_add_fusion = f32[256,128]{1,0:T(8,128)} fusion(f32[256,128]{1,0:T(8,128)S(1)} %bitcast.7, f32[256,128]{1,0:T(8,128)S(1)} %shard_map.82), kind=kLoop, calls=%fused_computation | loop fusion | flops 65536 | bytes 393216 | tf_op jit(solution)/shard_map/add | solution.py:291
Async XLA Ops:
  0.0 23.7 %copy-start = (f32[128,1,2,128]{3,2,1,0:T(2,128)S(1)}, f32[128,1,2,128]{3,2,1,0:T(2,128)}, u32[]{:S(2)}) copy-start(f32[128,1,2,128]{3,2,1,0:T(2,128)} %param.15) | copy-start | bytes 393220

commit v4 on v3

--- a/solution.py
+++ b/solution.py
@@ -7,7 +7,7 @@
 from jax.sharding import PartitionSpec as P
 
 scale_back = 4.0
-tile_batch = 32
+tile_batch = 48
 
 
 def partner(me, d, n):
@@ -81,12 +81,13 @@
     need_copy, fold_copy, cslot_copy, rslot_copy, dir_copy, weight_copy, tile_copy = fetched
 
     need_copy.wait()
-    sub = lax.broadcasted_iota(i32, (asks, side), 0)
+    lane = lax.broadcasted_iota(i32, (1, side), 1)
     for o in range(n_ex):
-        block = jnp.zeros((asks, side), i32)
+        line = jnp.zeros((1, side), i32)
         for j in range(asks):
-            block = jnp.where(sub == j, need_ref[0, o, j], block)
-        need_out[o] = block
+            line = jnp.where(lane == j, need_ref[0, o, j], line)
+        need_out[o] = line
+
     pl.semaphore_wait(barrier, n_ex - 1 + n_ft - 1)
 
     need_copies = exchange("ex", n_ex, ex_me, need_out, need_in, sems[0], sems[1])
@@ -128,7 +129,11 @@
     col_rows = dir_v.shape[0]
     for copy in need_copies:
         copy.wait()
-    asked = need_in[...]
+    asked = jnp.broadcast_to(need_in[...].astype(f32), (n_ex, asks, side))
+    sub = lax.broadcasted_iota(i32, (n_ex, asks, side), 1)
+    lane = lax.broadcasted_iota(i32, (n_ex, asks, side), 2)
+    asked = jnp.sum(jnp.where(sub == lane, asked, 0.0), axis=2, keepdims=True)
+    asked = jnp.broadcast_to(asked, (n_ex, asks, side)).astype(i32)
     asked = jnp.concatenate([asked * num_vecs + k for k in range(num_vecs)], axis=1)
     asked = asked.reshape(all_asks, side)
     lane = lax.broadcasted_iota(i32, (all_asks, side), 1)
@@ -265,8 +270,8 @@
         ] + [pltpu.SMEM(tile_cslot.shape, i32)] * 4 + [
             pltpu.VMEM(tiles.shape, bf16),
             pltpu.VMEM((col_blocks * num_vecs, side), f32),
-            pltpu.VMEM((n_ex, asks, side), i32),
-            pltpu.VMEM((n_ex, asks, side), i32),
+            pltpu.VMEM((n_ex, 1, side), i32),
+            pltpu.VMEM((n_ex, 1, side), i32),
             pltpu.VMEM((all_slots, width), i32),
             pltpu.VMEM((row_blocks + 8, width), f32),
             pltpu.VMEM((n_ft, row_blocks + 8, width), f32),

time: 24.5 us -> 24.3 us (level)
  Pallas kernels: 23 us -> 22.7 us
    pallas_call x1, Pallas kernels: 23 us -> 22.7 us  [local(): pl.pallas_call(functools.partial(kernel, n_ex, n_ft, num_vecs), out_shape...]
where the time goes in v4:
time: 24.3 us; the launch traced here: 24.1 us
  Pallas kernels  22.7 us (93%)
  between operations  0.7 us (3%)
  other arithmetic  0.67 us (3%)
    pallas_call x1, Pallas kernels, local(): pl.pallas_call(functools.partial(kernel, n_ex, n_ft, num_vecs), out_shape...  22.7 us
    add x1, other arithmetic, local(): return (own + scale_back * out).reshape(directions.shape)  0.67 us

profile of v4, /device:TPU:0, one launch (start us, length us, event | category | flops | bytes accessed | tf_op | source)
XLA Modules:
  0.0 24.1 jit_solution(11125444404370305297)
XLA Ops:
  0.0 0.0 copy-start
  0.7 22.7 %shard_map.82 = f32[256,128]{1,0:T(8,128)S(1)} custom-call(s32[1]{0:T(128)S(6)} %copy.10.count_ref, s32[96]{0:T(128)} %cslot_hbm.1, s32[96]{0:T(128)} %rslot_hbm.1, s32[1,4,8]{2,1,0:T(4,128)} %need_hbm.1, s32[1,4,8]{2,1,0:T(4,128)} %bitcast.9, f32[8,128]{1,0:T(8,128)} %bitcast.8, bf16[96,128,128]{2,1,0:T(8,128)(2,1)} %tiles_hbm.1, f32[256,128]{1,0:T(8,128)} %bitcast.6), custom_call_target="tpu_custom_call" | custom-call | tf_op jit(solution)/shard_map/pallas_call | solution.py:259
  23.4 0.0 copy-done
  23.4 0.7 %multiply_add_fusion = f32[256,128]{1,0:T(8,128)} fusion(f32[256,128]{1,0:T(8,128)S(1)} %bitcast.7, f32[256,128]{1,0:T(8,128)S(1)} %shard_map.82), kind=kLoop, calls=%fused_computation | loop fusion | flops 65536 | bytes 393216 | tf_op jit(solution)/shard_map/add | solution.py:296
Async XLA Ops:
  0.0 23.4 %copy-start = (f32[128,1,2,128]{3,2,1,0:T(2,128)S(1)}, f32[128,1,2,128]{3,2,1,0:T(2,128)}, u32[]{:S(2)}) copy-start(f32[128,1,2,128]{3,2,1,0:T(2,128)} %param.15) | copy-start | bytes 393220
